TPU v7x, 256 devices: a whole 4x4x8 slice. The times are simulated.
256 devices in a mesh: row: 32 (over x, z), col: 8 (over y, core).
Axes of the slice: x: 4, y: 4, z: 8, core: 2. Of those that a mesh axis runs over, the one named last changes fastest.
Arguments:
- mom_a: float32 [1536, 12288], P('row', 'col'), may hold values from -6 to 6
- grad_a: float32 [1536, 12288], P('row', 'col'), may hold values from -6 to 6
- basis_a: float32 [512, 12288], P('row', 'col'), may hold values from -0.0546875 to 0.0546875
- mom_b: float32 [7168, 1536], P('row', 'col'), may hold values from -6 to 6
- grad_b: float32 [7168, 1536], P('row', 'col'), may hold values from -6 to 6
- basis_b: float32 [512, 1536], P('row', 'col'), may hold values from -0.15625 to 0.15625
Outputs:
- new_mom_a: float32 [1536, 12288], P('row', 'col')
- update_a: bfloat16 [1536, 12288], P('row', 'col')
- new_basis_a: float32 [512, 12288], P('row', 'col')
- new_mom_b: float32 [7168, 1536], P('row', 'col')
- update_b: bfloat16 [7168, 1536], P('row', 'col')
- new_basis_b: float32 [512, 1536], P('row', 'col')
All inputs are finite; a program needn't handle non-finite values.
Results may differ from a plain program's by a relative error of at most 0.0049.
Values sent between devices are 32-bit elements; how exact they have to be, the bound alone decides.
No kernel may reach another device: no remote copies, remote signals or barrier semaphores. Data moves between devices by JAX's collectives and lax.ppermute only.
A program may use at most 64 MiB of HBM per device.

v0:
```python
import math
import jax
import jax.numpy as jnp
from jax import lax
from jax.sharding import PartitionSpec as P

MU = 0.95
EPS = 1e-06


def sent_to_all(array, axis):
    size = lax.axis_size(axis)
    return lax.all_to_all(
        jnp.broadcast_to(array[None], (size, *array.shape)), axis, 0, 0, tiled=True
    )


def over_copies(array, axis):
    everything = sent_to_all(array, axis)
    return jnp.sum(everything, axis=0)


def split_up(array, dim, size):
    before, after = (array.shape[:dim], array.shape[dim + 1 :])
    return jnp.moveaxis(array.reshape(*before, size, -1, *after), dim, 0)


def summed_on_arrival(array, axis, dim):
    size = lax.axis_size(axis)
    parts = lax.all_to_all(split_up(array, dim, size), axis, 0, 0, tiled=True)
    return jnp.sum(parts, axis=0)


def in_one_piece(arrays, axis, dim, along):
    widths = [a.shape[along] for a in arrays]
    both = jnp.concatenate(arrays, axis=along)
    whole = lax.all_gather(both, axis, axis=dim, tiled=True)
    return tuple(jnp.split(whole, [sum(widths[:k]) for k in range(1, len(widths))], axis=along))


def together(arrays, axis):
    ends = [0]
    for a in arrays:
        ends.append(ends[-1] + a.size)
    so_far = lax.psum(jnp.concatenate([a.ravel() for a in arrays]), axis)
    return tuple((so_far[b:e].reshape(a.shape) for a, b, e in zip(arrays, ends, ends[1:])))


def project(buffer, basis):
    partial_proj = jnp.dot(
        buffer,
        lax.all_gather(basis, "row", axis=0, tiled=True).T,
        precision=lax.Precision.HIGHEST,
        preferred_element_type=jnp.float32,
    )
    return over_copies(partial_proj, "col")


def local_gram(proj):
    return jnp.dot(
        proj.T, proj, precision=lax.Precision.HIGHEST, preferred_element_type=jnp.float32
    )


def finish(buffer, proj, gram):
    highest = lax.Precision.HIGHEST
    lower = jnp.linalg.cholesky(gram)
    ortho = lax.linalg.triangular_solve(lower, proj, left_side=False, lower=True, transpose_a=True)
    rank = ortho.shape[1]
    share = summed_on_arrival(
        jnp.dot(ortho.T, buffer, precision=highest, preferred_element_type=jnp.float32), "row", 0
    )
    squares = over_copies(jnp.sum(share * share, axis=1, keepdims=True), "col")
    norms = jnp.sqrt(squares + EPS)
    own_basis = share / norms
    full_basis, full_norms = in_one_piece((own_basis, norms), "row", 0, 1)
    trans = full_basis * full_norms
    new_mom = buffer - (1.0 - MU) * jnp.dot(
        ortho, trans, precision=highest, preferred_element_type=jnp.float32
    )
    total_rows = buffer.shape[0] * lax.axis_size("row")
    total_cols = buffer.shape[1] * lax.axis_size("col")
    scale = math.sqrt(total_rows * total_cols / rank)
    update = (
        jnp.dot(ortho, full_basis, precision=highest, preferred_element_type=jnp.float32) * scale
    ).astype(jnp.bfloat16)
    return (new_mom, update, own_basis)


def shards(mom_a, grad_a, basis_a, mom_b, grad_b, basis_b):
    buffers = [MU * mom_a + grad_a, MU * mom_b + grad_b]
    projs = [project(buffers[0], basis_a), project(buffers[1], basis_b)]
    grams = together((local_gram(projs[0]), local_gram(projs[1])), "row")
    first = finish(buffers[0], projs[0], grams[0])
    second = finish(buffers[1], projs[1], grams[1])
    return (first[0], first[1], first[2], second[0], second[1], second[2])


def solution(mesh):
    return jax.shard_map(
        shards,
        mesh=mesh,
        in_specs=(
            P("row", "col"),
            P("row", "col"),
            P("row", "col"),
            P("row", "col"),
            P("row", "col"),
            P("row", "col"),
        ),
        out_specs=(
            P("row", "col"),
            P("row", "col"),
            P("row", "col"),
            P("row", "col"),
            P("row", "col"),
            P("row", "col"),
        ),
        check_vma=False,
    )
```

profile of v0, /device:TPU:8, one launch (start us, length us, event | category | flops | bytes accessed | tf_op | source)
XLA Modules:
  0.0 711.3 jit_solution(5581359570950233791)
XLA Ops:
  7.9 52.6 %all_gather.13 = f32[512,192]{1,0:T(8,128)S(1)} all-gather(f32[16,192]{1,0:T(8,128)} %param.12), channel_id=1, replica_groups=mesh['row'=32,'col'=8] {'row'}, dimensions={0}, use_global_device_ids=true | all-gather | bytes 405504 | tf_op jit(solution)/shard_map/all_gather | solution.py:52
  69.8 23.7 %all-gather.3.cloned.1.call-done = f32[512,1536]{1,0:T(8,128)} async-done(((f32[16,1536]{1,0:T(8,128)}), f32[512,1536]{1,0:T(8,128)}) %all-gather.3.cloned.1.call-update) | async-done | bytes 3145744 | tf_op jit(solution)/shard_map/all_gather | solution.py:52
  98.4 14.1 %all-to-all-done.1 = f32[8,224,512]{2,1,0:T(8,128)} async-done(((f32[8,224,512]{2,1,0:T(8,128)}), f32[8,224,512]{2,1,0:T(8,128)}, u32[]{:S(2)}, u32[]{:S(2)}) %all-to-all-start.1) | async-done | bytes 3670048 | tf_op jit(solution)/shard_map/all_to_all | solution.py:13
  133.0 151.3 %all-reduce.3.cloned.1.call-done = f32[524288]{0:T(1024)} async-done(((f32[524288]{0:T(1024)}), f32[524288]{0:T(1024)}) %all-reduce.3.cloned.1.call-update) | async-done | bytes 2097168 | tf_op jit(solution)/shard_map/psum | solution.py:45
  287.7 11.7 %cholesky.286 = f32[128,128]{1,0:T(8,128)S(1)} custom-call(f32[128,128]{1,0:T(8,128)S(1)} %cholesky.426), custom_call_target="Cholesky" | custom-call | tf_op jit(solution)/shard_map/jit(cholesky)/cholesky | solution.py:67
  299.5 9.8 %custom-call.31 = f32[1,128,128]{1,2,0:T(8,128)S(1)} custom-call(f32[1,128,128]{2,1,0:T(8,128)S(1)} %get-tuple-element.64), custom_call_target="InvertDiagBlocksLowerTriangular" | custom-call | tf_op jit(solution)/shard_map/jit(cholesky)/cholesky | solution.py:67
  310.1 11.9 %cholesky.305 = f32[128,128]{1,0:T(8,128)S(1)} custom-call(f32[128,128]{1,0:T(8,128)S(1)} %cholesky.430), custom_call_target="Cholesky" | custom-call | tf_op jit(solution)/shard_map/jit(cholesky)/cholesky | solution.py:67
  322.0 9.8 %custom-call.32 = f32[1,128,128]{1,2,0:T(8,128)S(1)} custom-call(f32[1,128,128]{2,1,0:T(8,128)S(1)} %get-tuple-element.61), custom_call_target="InvertDiagBlocksLowerTriangular" | custom-call | tf_op jit(solution)/shard_map/jit(cholesky)/cholesky | solution.py:67
  332.5 11.7 %cholesky.326 = f32[128,128]{1,0:T(8,128)S(1)} custom-call(f32[128,128]{1,0:T(8,128)S(1)} %cholesky.435), custom_call_target="Cholesky" | custom-call | tf_op jit(solution)/shard_map/jit(cholesky)/cholesky | solution.py:67
  344.9 9.8 %custom-call.33 = f32[1,128,128]{1,2,0:T(8,128)S(1)} custom-call(f32[1,128,128]{2,1,0:T(8,128)S(1)} %get-tuple-element.58), custom_call_target="InvertDiagBlocksLowerTriangular" | custom-call | tf_op jit(solution)/shard_map/jit(cholesky)/cholesky | solution.py:67
  355.3 11.9 %cholesky.343 = f32[128,128]{1,0:T(8,128)S(1)} custom-call(f32[128,128]{1,0:T(8,128)S(1)} %convolution_subtract_fusion.8), custom_call_target="Cholesky" | custom-call | tf_op jit(solution)/shard_map/jit(cholesky)/cholesky | solution.py:67
  371.3 8.0 %while.2 = (s32[]{:T(128)}, f32[512,512]{1,0:T(8,128)S(1)}, s32[4,2]{0,1:T(2,128)S(1)}, f32[4,128,128]{2,1,0:T(8,128)S(1)}, s32[]{:T(128)}) while((s32[]{:T(128)}, f32[512,512]{1,0:T(8,128)S(1)}, s32[4,2]{0,1:T(2,128)S(1)}, f32[4,128,128]{2,1,0:T(8,128)S(1)}, s32[]{:T(128)}) %tuple.57), condition=%wide.while_cond, body=%wide.while_body.sunk | while | flops 2 | bytes 131181 | solution.py:68
  379.3 39.3 %custom-call.26 = f32[4,128,128]{1,2,0:T(8,128)S(1)} custom-call(f32[4,128,128]{2,1,0:T(8,128)S(1)} %get-tuple-element.14), custom_call_target="InvertDiagBlocksLowerTriangular" | custom-call | tf_op jit(solution)/shard_map/triangular_solve | solution.py:68
  439.6 12.5 %cholesky.358 = f32[128,128]{1,0:T(8,128)S(1)} custom-call(f32[128,128]{1,0:T(8,128)} %cholesky.439), custom_call_target="Cholesky" | custom-call | tf_op jit(solution)/shard_map/jit(cholesky)/cholesky | solution.py:67
  452.8 11.3 %custom-call.34 = f32[1,128,128]{1,2,0:T(8,128)} custom-call(f32[1,128,128]{2,1,0:T(8,128)} %get-tuple-element.54), custom_call_target="InvertDiagBlocksLowerTriangular" | custom-call | tf_op jit(solution)/shard_map/jit(cholesky)/cholesky | solution.py:67
  469.7 12.5 %cholesky.377 = f32[128,128]{1,0:T(8,128)S(1)} custom-call(f32[128,128]{1,0:T(8,128)} %cholesky.443), custom_call_target="Cholesky" | custom-call | tf_op jit(solution)/shard_map/jit(cholesky)/cholesky | solution.py:67
  482.9 10.8 %custom-call.35 = f32[1,128,128]{1,2,0:T(8,128)S(1)} custom-call(f32[1,128,128]{2,1,0:T(8,128)} %get-tuple-element.51), custom_call_target="InvertDiagBlocksLowerTriangular" | custom-call | tf_op jit(solution)/shard_map/jit(cholesky)/cholesky | solution.py:67
  498.3 12.5 %cholesky.398 = f32[128,128]{1,0:T(8,128)S(1)} custom-call(f32[128,128]{1,0:T(8,128)} %cholesky.448), custom_call_target="Cholesky" | custom-call | tf_op jit(solution)/shard_map/jit(cholesky)/cholesky | solution.py:67
  511.5 10.6 %custom-call.36 = f32[1,128,128]{1,2,0:T(8,128)S(1)} custom-call(f32[1,128,128]{2,1,0:T(8,128)} %get-tuple-element.48), custom_call_target="InvertDiagBlocksLowerTriangular" | custom-call | tf_op jit(solution)/shard_map/jit(cholesky)/cholesky | solution.py:67
  532.5 12.5 %cholesky.415 = f32[128,128]{1,0:T(8,128)S(1)} custom-call(f32[128,128]{1,0:T(8,128)} %convolution_subtract_fusion.7), custom_call_target="Cholesky" | custom-call | tf_op jit(solution)/shard_map/jit(cholesky)/cholesky | solution.py:67
  559.9 39.3 %custom-call.27 = f32[4,128,128]{1,2,0:T(8,128)S(1)} custom-call(f32[4,128,128]{2,1,0:T(8,128)S(1)} %get-tuple-element.22), custom_call_target="InvertDiagBlocksLowerTriangular" | custom-call | tf_op jit(solution)/shard_map/triangular_solve | solution.py:68
  602.4 31.5 %all_to_all.30 = f32[32,16,192]{2,1,0:T(8,128)S(1)} all-to-all(f32[32,16,192]{2,1,0:T(8,128)S(1)} %bitcast.117), channel_id=1, replica_groups=mesh['row'=32,'col'=8] {'row'}, dimensions={0} | all-to-all | bytes 786432 | tf_op jit(solution)/shard_map/all_to_all | solution.py:30
  634.0 8.8 %all_to_all.31 = f32[8,16,1]{1,2,0:T(1,128)S(1)} all-to-all(f32[8,16,1]{1,2,0:T(1,128)S(1)} %broadcast_in_dim.12), channel_id=1, replica_groups=mesh['row'=32,'col'=8] {'col'}, dimensions={0} | all-to-all | bytes 1024 | tf_op jit(solution)/shard_map/all_to_all | solution.py:13
  643.1 49.0 %all_gather.15 = f32[512,193]{1,0:T(8,128)S(1)} all-gather(f32[16,193]{1,0:T(8,128)S(1)} %pad_maximum_fusion.10), channel_id=1, replica_groups=mesh['row'=32,'col'=8] {'row'}, dimensions={0}, use_global_device_ids=true | all-gather | bytes 407616 | tf_op jit(solution)/shard_map/all_gather | solution.py:37
  (177 shorter events, 130.0 us)
Async XLA Ops:
  7.2 86.4 %all-gather.3.cloned.1.call-start = ((), (), s32[]{:S(2)}) async-start(), calls=%async_computation.6 | async-start | bytes 3244032 | tf_op jit(solution)/shard_map/all_gather | solution.py:52
  64.9 28.7 %copy-start.4 = (f32[48,1536]{1,0:T(8,128)S(1)}, f32[48,1536]{1,0:T(8,128)}, u32[]{:S(2)}) copy-start(f32[48,1536]{1,0:T(8,128)} %param.8) | copy-start | bytes 884740
  64.9 28.7 %copy-start.5 = (f32[48,1536]{1,0:T(8,128)S(1)}, f32[48,1536]{1,0:T(8,128)}, u32[]{:S(2)}) copy-start(f32[48,1536]{1,0:T(8,128)} %param.7) | copy-start | bytes 884740
  64.9 47.7 %all-to-all-start.1 = ((f32[8,224,512]{2,1,0:T(8,128)}), f32[8,224,512]{2,1,0:T(8,128)}, u32[]{:S(2)}, u32[]{:S(2)}) async-start(f32[8,224,512]{2,1,0:T(8,128)} %broadcast_in_dim.10), calls=%async_computation.1 | async-start | bytes 7340032 | tf_op jit(solution)/shard_map/all_to_all | solution.py:13
  113.5 16.6 %all-to-all-start = ((f32[8,48,512]{2,1,0:T(8,128)}), f32[8,48,512]{2,1,0:T(8,128)S(1)}, u32[]{:S(2)}, u32[]{:S(2)}) async-start(f32[8,48,512]{2,1,0:T(8,128)} %broadcast_in_dim.8), calls=%async_computation | async-start | bytes 1572864 | tf_op jit(solution)/shard_map/all_to_all | solution.py:13
  118.4 165.9 %all-reduce.3.cloned.1.call-start = ((), (), s32[]{:S(2)}) async-start(), calls=%async_computation.7 | async-start | bytes 4194304 | tf_op jit(solution)/shard_map/psum | solution.py:45
  121.5 10.1 %copy-start.1 = (f32[224,512]{1,0:T(8,128)}, f32[224,512]{1,0:T(8,128)S(1)}, u32[]{:S(2)}) copy-start(f32[224,512]{1,0:T(8,128)S(1)} %reduce_sum.73) | copy-start | bytes 1376260
  418.8 6.7 copy-start.9
  419.2 6.3 copy-start.11
  419.7 5.9 copy-start.14
  425.6 100.3 %all-to-all-start.2 = ((f32[32,16,1536]{2,1,0:T(8,128)}), f32[32,16,1536]{2,1,0:T(8,128)S(1)}, u32[]{:S(2)}, u32[]{:S(2)}) async-start(f32[32,16,1536]{2,1,0:T(8,128)} %bitcast.114), calls=%async_computation.2 | async-start | bytes 6291456 | tf_op jit(solution)/shard_map/all_to_all | solution.py:30
  526.0 73.2 %copy-start.2 = (f32[224,512]{1,0:T(8,128)S(1)}, f32[224,512]{1,0:T(8,128)}, u32[]{:S(2)}) copy-start(f32[224,512]{1,0:T(8,128)} %copy-done.1) | copy-start | bytes 1376260
  526.8 19.5 %all-to-all-start.3 = ((f32[8,16,1]{1,2,0:T(1,128)}), f32[8,16,1]{1,2,0:T(1,128)S(1)}, u32[]{:S(2)}, u32[]{:S(2)}) async-start(f32[8,16,1]{1,2,0:T(1,128)} %broadcast_in_dim.11), calls=%async_computation.3 | async-start | bytes 8192 | tf_op jit(solution)/shard_map/all_to_all | solution.py:13
  531.6 164.2 %all-gather.5.cloned.1.call-start = ((), (), s32[]{:S(2)}) async-start(), calls=%async_computation.8 | async-start | bytes 3514368 | tf_op jit(solution)/shard_map/all_gather | solution.py:37
  546.5 54.6 %copy-start.19 = (f32[16,1536]{1,0:T(8,128)}, f32[16,1536]{1,0:T(8,128)S(1)}, u32[]{:S(2)}) copy-start(f32[16,1536]{1,0:T(8,128)S(1)} %broadcast_divide_fusion) | copy-start | bytes 294916
  547.2 54.1 %copy-start.7 = (f32[224,192]{0,1:T(8,128)S(1)}, f32[224,192]{0,1:T(8,128)}, u32[]{:S(2)}) copy-start(f32[224,192]{0,1:T(8,128)} %param.11) | copy-start | bytes 516100
  547.2 54.1 %copy-start.8 = (f32[224,192]{0,1:T(8,128)S(1)}, f32[224,192]{0,1:T(8,128)}, u32[]{:S(2)}) copy-start(f32[224,192]{0,1:T(8,128)} %param.10) | copy-start | bytes 516100
  601.3 94.4 %copy-start.10 = (f32[48,128]{1,0:T(8,128)S(1)}, f32[48,128]{1,0:T(8,128)}, u32[]{:S(2)}) copy-start(f32[48,128]{1,0:T(8,128)} %copy-done.9) | copy-start | bytes 73732
  601.4 94.4 %copy-start.12 = (f32[48,128]{1,0:T(8,128)S(1)}, f32[48,128]{1,0:T(8,128)}, u32[]{:S(2)}) copy-start(f32[48,128]{1,0:T(8,128)} %copy-done.11) | copy-start | bytes 73732
  601.4 94.4 %copy-start.15 = (f32[48,128]{1,0:T(8,128)S(1)}, f32[48,128]{1,0:T(8,128)}, u32[]{:S(2)}) copy-start(f32[48,128]{1,0:T(8,128)} %copy-done.14) | copy-start | bytes 73732
  601.4 94.4 %copy-start.18 = (f32[48,128]{1,0:T(8,128)S(1)}, f32[48,128]{1,0:T(8,128)}, u32[]{:S(2)}) copy-start(f32[48,128]{1,0:T(8,128)} %copy-done.17) | copy-start | bytes 73732
  643.0 57.5 %copy-start.20 = (f32[16,192]{1,0:T(8,128)}, f32[16,192]{1,0:T(8,128)S(1)}, u32[]{:S(2)}) copy-start(f32[16,192]{1,0:T(8,128)S(1)} %broadcast_divide_fusion.1) | copy-start | bytes 36868
  692.3 9.2 %copy-start.6 = (f32[48,1536]{1,0:T(8,128)S(1)}, f32[48,1536]{1,0:T(8,128)}, u32[]{:S(2)}) copy-start(f32[48,1536]{1,0:T(8,128)} %param.7) | copy-start | bytes 884740
  695.8 5.8 copy-start
  (4 other events, 7.6 us)
Sparse Core Ops, SparseCore 0:
  10.6 82.9 all-gather.2
  133.1 151.1 all-reduce.2
  547.3 89.6 all-gather.4
where the time goes:
time: 717 us; the launch traced here: 711 us
  other arithmetic  254 us (35%)
  waiting for transfers between devices  197 us (27%)
  blocking collectives  142 us (20%)
  matrix products  41.9 us (6%)
  local copies, waits for them, and re-layouts  35.4 us (5%)
  starting transfers between devices  21.2 us (3%)
  between operations  19.9 us (3%)
    another operation x28, other arithmetic, finish(): lower = jnp.linalg.cholesky(gram)  166 us
    psum x1, waiting for transfers between devices, together(): so_far = lax.psum(jnp.concatenate([a.ravel() for a in arrays]), axis)  151 us
    another operation x5, other arithmetic, finish(): lax.linalg.triangular_solve(lower, proj, left_side=False, lower=True, tra...  80.1 us
    all_gather x1, blocking collectives, project(): lax.all_gather(basis, 'row', axis=0, tiled=True)  52.6 us
    all_gather x1, blocking collectives, in_one_piece(): whole = lax.all_gather(both, axis, axis=dim, tiled=True)  49 us
    all_to_all x1, blocking collectives, summed_on_arrival(): parts = lax.all_to_all(split_up(array, dim, size), axis, 0, 0, tiled=True)  31.5 us
    all_gather x1, waiting for transfers between devices, project(): lax.all_gather(basis, 'row', axis=0, tiled=True)  23.7 us
    all_to_all x3, waiting for transfers between devices, sent_to_all(): lax.all_to_all(jnp.broadcast_to(array[None], (size, *array.shape)), axis,...  21.4 us
  transfers between devices with their start and end apart: 7, of which 4 were waited for; matrix products, arithmetic and copies ran while one was open for 25% of the time, Pallas kernels for 0%

commit v1 on v0

--- a/solution.py
+++ b/solution.py
@@ -49,7 +49,9 @@
 def project(buffer, basis):
     partial_proj = jnp.dot(
         buffer,
-        lax.all_gather(basis, "row", axis=0, tiled=True).T,
+        jnp.concatenate(
+            lax.all_to_all(jnp.stack([basis] * lax.axis_size("row")), "row", 0, 0), axis=0
+        ).T,
         precision=lax.Precision.HIGHEST,
         preferred_element_type=jnp.float32,
     )

time: 717 us -> 774 us (1.079)
  waiting for transfers between devices: 197 us -> 267 us
  blocking collectives: 142 us -> 117 us
    all_to_all x0 -> x1, waiting for transfers between devices: none -> 71.1 us  [project(): lax.all_to_all(jnp.stack([basis] * lax.axis_size('row')), 'row', 0, 0)]
    all_gather x1 -> x0, blocking collectives: 52.6 us -> none  [project(): lax.all_gather(basis, 'row', axis=0, tiled=True)]
    all_to_all x0 -> x1, blocking collectives: none -> 28.1 us  [project(): lax.all_to_all(jnp.stack([basis] * lax.axis_size('row')), 'row', 0, 0)]
    all_to_all x3, waiting for transfers between devices: 21.4 us -> 46 us  [sent_to_all(): lax.all_to_all(jnp.broadcast_to(array[None], (size, *array.shape)), axis,...]
    all_gather x1 -> x0, waiting for transfers between devices: 23.7 us -> none  [project(): lax.all_gather(basis, 'row', axis=0, tiled=True)]
    another operation x24 -> x26, local copies, waits for them, and re-layouts: 15.8 us -> 19.5 us
  transfers between devices with their start and end apart: 7 -> 7, of which waited for: 4 -> 4; matrix products, arithmetic and copies ran while one was open for 25% -> 23% of each run, Pallas kernels for 0% -> 0%
where the time goes in v1:
time: 774 us; the launch traced here: 768 us
  waiting for transfers between devices  267 us (34%)
  other arithmetic  254 us (33%)
  blocking collectives  117 us (15%)
  matrix products  41.8 us (5%)
  local copies, waits for them, and re-layouts  40.2 us (5%)
  starting transfers between devices  27 us (3%)
  between operations  20.2 us (3%)
    another operation x28, other arithmetic, finish(): lower = jnp.linalg.cholesky(gram)  166 us
    psum x1, waiting for transfers between devices, together(): so_far = lax.psum(jnp.concatenate([a.ravel() for a in arrays]), axis)  150 us
    another operation x5, other arithmetic, finish(): lax.linalg.triangular_solve(lower, proj, left_side=False, lower=True, tra...  80.1 us
    all_to_all x1, waiting for transfers between devices, project(): lax.all_to_all(jnp.stack([basis] * lax.axis_size('row')), 'row', 0, 0)  71.1 us
    all_gather x1, blocking collectives, in_one_piece(): whole = lax.all_gather(both, axis, axis=dim, tiled=True)  49 us
    all_to_all x3, waiting for transfers between devices, sent_to_all(): lax.all_to_all(jnp.broadcast_to(array[None], (size, *array.shape)), axis,...  46 us
    all_to_all x1, blocking collectives, summed_on_arrival(): parts = lax.all_to_all(split_up(array, dim, size), axis, 0, 0, tiled=True)  31.7 us
    all_to_all x1, blocking collectives, project(): lax.all_to_all(jnp.stack([basis] * lax.axis_size('row')), 'row', 0, 0)  28.1 us
  transfers between devices with their start and end apart: 7, of which 4 were waited for; matrix products, arithmetic and copies ran while one was open for 23% of the time, Pallas kernels for 0%

profile of v1, /device:TPU:8, one launch (start us, length us, event | category | flops | bytes accessed | tf_op | source)
XLA Modules:
  0.0 767.6 jit_solution(11073341572894060549)
XLA Ops:
  7.9 28.1 %all_to_all.40 = f32[32,16,192]{2,1,0:T(8,128)} all-to-all(f32[32,16,192]{2,1,0:T(8,128)S(1)} %stack.5), channel_id=1, replica_groups=mesh['row'=32,'col'=8] {'row'}, dimensions={0} | all-to-all | bytes 786432 | tf_op jit(solution)/shard_map/all_to_all | solution.py:53
  47.5 71.1 %all-to-all-done = f32[32,16,1536]{2,1,0:T(8,128)S(1)} async-done(((f32[32,16,1536]{2,1,0:T(8,128)}), f32[32,16,1536]{2,1,0:T(8,128)S(1)}, u32[]{:S(2)}, u32[]{:S(2)}) %all-to-all-start) | async-done | bytes 3145760 | tf_op jit(solution)/shard_map/all_to_all | solution.py:53
  131.0 38.7 %all-to-all-done.3 = f32[8,224,512]{2,1,0:T(8,128)} async-done(((f32[8,224,512]{2,1,0:T(8,128)}), f32[8,224,512]{2,1,0:T(8,128)}, u32[]{:S(2)}, u32[]{:S(2)}) %all-to-all-start.3) | async-done | bytes 3670048 | tf_op jit(solution)/shard_map/all_to_all | solution.py:13
  190.2 150.2 %all-reduce.3.cloned.1.call-done = f32[524288]{0:T(1024)} async-done(((f32[524288]{0:T(1024)}), f32[524288]{0:T(1024)}) %all-reduce.3.cloned.1.call-update) | async-done | bytes 2097168 | tf_op jit(solution)/shard_map/psum | solution.py:45
  343.8 11.7 %cholesky.286 = f32[128,128]{1,0:T(8,128)S(1)} custom-call(f32[128,128]{1,0:T(8,128)S(1)} %cholesky.426), custom_call_target="Cholesky" | custom-call | tf_op jit(solution)/shard_map/jit(cholesky)/cholesky | solution.py:69
  355.5 9.8 %custom-call.31 = f32[1,128,128]{1,2,0:T(8,128)S(1)} custom-call(f32[1,128,128]{2,1,0:T(8,128)S(1)} %get-tuple-element.64), custom_call_target="InvertDiagBlocksLowerTriangular" | custom-call | tf_op jit(solution)/shard_map/jit(cholesky)/cholesky | solution.py:69
  366.1 11.9 %cholesky.305 = f32[128,128]{1,0:T(8,128)S(1)} custom-call(f32[128,128]{1,0:T(8,128)S(1)} %cholesky.430), custom_call_target="Cholesky" | custom-call | tf_op jit(solution)/shard_map/jit(cholesky)/cholesky | solution.py:69
  378.0 9.8 %custom-call.32 = f32[1,128,128]{1,2,0:T(8,128)S(1)} custom-call(f32[1,128,128]{2,1,0:T(8,128)S(1)} %get-tuple-element.61), custom_call_target="InvertDiagBlocksLowerTriangular" | custom-call | tf_op jit(solution)/shard_map/jit(cholesky)/cholesky | solution.py:69
  388.5 11.7 %cholesky.326 = f32[128,128]{1,0:T(8,128)S(1)} custom-call(f32[128,128]{1,0:T(8,128)S(1)} %cholesky.435), custom_call_target="Cholesky" | custom-call | tf_op jit(solution)/shard_map/jit(cholesky)/cholesky | solution.py:69
  400.9 9.8 %custom-call.33 = f32[1,128,128]{1,2,0:T(8,128)S(1)} custom-call(f32[1,128,128]{2,1,0:T(8,128)S(1)} %get-tuple-element.58), custom_call_target="InvertDiagBlocksLowerTriangular" | custom-call | tf_op jit(solution)/shard_map/jit(cholesky)/cholesky | solution.py:69
  411.3 11.9 %cholesky.343 = f32[128,128]{1,0:T(8,128)S(1)} custom-call(f32[128,128]{1,0:T(8,128)S(1)} %convolution_subtract_fusion.8), custom_call_target="Cholesky" | custom-call | tf_op jit(solution)/shard_map/jit(cholesky)/cholesky | solution.py:69
  427.3 8.0 %while.2 = (s32[]{:T(128)}, f32[512,512]{1,0:T(8,128)S(1)}, s32[4,2]{0,1:T(2,128)S(1)}, f32[4,128,128]{2,1,0:T(8,128)S(1)}, s32[]{:T(128)}) while((s32[]{:T(128)}, f32[512,512]{1,0:T(8,128)S(1)}, s32[4,2]{0,1:T(2,128)S(1)}, f32[4,128,128]{2,1,0:T(8,128)S(1)}, s32[]{:T(128)}) %tuple.57), condition=%wide.while_cond, body=%wide.while_body.sunk | while | flops 2 | bytes 131181 | solution.py:70
  435.3 39.3 %custom-call.26 = f32[4,128,128]{1,2,0:T(8,128)S(1)} custom-call(f32[4,128,128]{2,1,0:T(8,128)S(1)} %get-tuple-element.14), custom_call_target="InvertDiagBlocksLowerTriangular" | custom-call | tf_op jit(solution)/shard_map/triangular_solve | solution.py:70
  495.7 12.5 %cholesky.358 = f32[128,128]{1,0:T(8,128)S(1)} custom-call(f32[128,128]{1,0:T(8,128)} %cholesky.439), custom_call_target="Cholesky" | custom-call | tf_op jit(solution)/shard_map/jit(cholesky)/cholesky | solution.py:69
  508.9 11.3 %custom-call.34 = f32[1,128,128]{1,2,0:T(8,128)} custom-call(f32[1,128,128]{2,1,0:T(8,128)} %get-tuple-element.54), custom_call_target="InvertDiagBlocksLowerTriangular" | custom-call | tf_op jit(solution)/shard_map/jit(cholesky)/cholesky | solution.py:69
  525.8 12.5 %cholesky.377 = f32[128,128]{1,0:T(8,128)S(1)} custom-call(f32[128,128]{1,0:T(8,128)} %cholesky.443), custom_call_target="Cholesky" | custom-call | tf_op jit(solution)/shard_map/jit(cholesky)/cholesky | solution.py:69
  539.0 10.8 %custom-call.35 = f32[1,128,128]{1,2,0:T(8,128)S(1)} custom-call(f32[1,128,128]{2,1,0:T(8,128)} %get-tuple-element.51), custom_call_target="InvertDiagBlocksLowerTriangular" | custom-call | tf_op jit(solution)/shard_map/jit(cholesky)/cholesky | solution.py:69
  554.4 12.5 %cholesky.398 = f32[128,128]{1,0:T(8,128)S(1)} custom-call(f32[128,128]{1,0:T(8,128)} %cholesky.448), custom_call_target="Cholesky" | custom-call | tf_op jit(solution)/shard_map/jit(cholesky)/cholesky | solution.py:69
  567.6 10.6 %custom-call.36 = f32[1,128,128]{1,2,0:T(8,128)S(1)} custom-call(f32[1,128,128]{2,1,0:T(8,128)} %get-tuple-element.48), custom_call_target="InvertDiagBlocksLowerTriangular" | custom-call | tf_op jit(solution)/shard_map/jit(cholesky)/cholesky | solution.py:69
  588.5 12.5 %cholesky.415 = f32[128,128]{1,0:T(8,128)S(1)} custom-call(f32[128,128]{1,0:T(8,128)} %convolution_subtract_fusion.7), custom_call_target="Cholesky" | custom-call | tf_op jit(solution)/shard_map/jit(cholesky)/cholesky | solution.py:69
  616.0 39.3 %custom-call.27 = f32[4,128,128]{1,2,0:T(8,128)S(1)} custom-call(f32[4,128,128]{2,1,0:T(8,128)S(1)} %get-tuple-element.22), custom_call_target="InvertDiagBlocksLowerTriangular" | custom-call | tf_op jit(solution)/shard_map/triangular_solve | solution.py:70
  658.5 31.7 %all_to_all.41 = f32[32,16,192]{2,1,0:T(8,128)S(1)} all-to-all(f32[32,16,192]{2,1,0:T(8,128)S(1)} %bitcast.121), channel_id=1, replica_groups=mesh['row'=32,'col'=8] {'row'}, dimensions={0} | all-to-all | bytes 786432 | tf_op jit(solution)/shard_map/all_to_all | solution.py:30
  690.3 8.5 %all_to_all.42 = f32[8,16,1]{1,2,0:T(1,128)S(1)} all-to-all(f32[8,16,1]{1,2,0:T(1,128)S(1)} %broadcast_in_dim.12), channel_id=1, replica_groups=mesh['row'=32,'col'=8] {'col'}, dimensions={0} | all-to-all | bytes 1024 | tf_op jit(solution)/shard_map/all_to_all | solution.py:13
  699.1 49.0 %all_gather.7 = f32[512,193]{1,0:T(8,128)S(1)} all-gather(f32[16,193]{1,0:T(8,128)S(1)} %pad_maximum_fusion.10), channel_id=1, replica_groups=mesh['row'=32,'col'=8] {'row'}, dimensions={0}, use_global_device_ids=true | all-gather | bytes 407616 | tf_op jit(solution)/shard_map/all_gather | solution.py:37
  (180 shorter events, 139.8 us)
Async XLA Ops:
  38.9 5.8 copy-start.6
  38.9 5.8 copy-start.8
  38.9 79.7 %all-to-all-start = ((f32[32,16,1536]{2,1,0:T(8,128)}), f32[32,16,1536]{2,1,0:T(8,128)S(1)}, u32[]{:S(2)}, u32[]{:S(2)}) async-start(f32[32,16,1536]{2,1,0:T(8,128)} %stack.4), calls=%async_computation | async-start | bytes 6291456 | tf_op jit(solution)/shard_map/all_to_all | solution.py:53
  121.9 47.8 %all-to-all-start.3 = ((f32[8,224,512]{2,1,0:T(8,128)}), f32[8,224,512]{2,1,0:T(8,128)}, u32[]{:S(2)}, u32[]{:S(2)}) async-start(f32[8,224,512]{2,1,0:T(8,128)} %broadcast_in_dim.10), calls=%async_computation.3 | async-start | bytes 7340032 | tf_op jit(solution)/shard_map/all_to_all | solution.py:13
  170.7 16.6 %all-to-all-start.1 = ((f32[8,48,512]{2,1,0:T(8,128)}), f32[8,48,512]{2,1,0:T(8,128)S(1)}, u32[]{:S(2)}, u32[]{:S(2)}) async-start(f32[8,48,512]{2,1,0:T(8,128)} %broadcast_in_dim.8), calls=%async_computation.1 | async-start | bytes 1572864 | tf_op jit(solution)/shard_map/all_to_all | solution.py:13
  175.6 164.8 %all-reduce.3.cloned.1.call-start = ((), (), s32[]{:S(2)}) async-start(), calls=%async_computation.8 | async-start | bytes 4194304 | tf_op jit(solution)/shard_map/psum | solution.py:45
  178.6 10.1 %copy-start.1 = (f32[224,512]{1,0:T(8,128)}, f32[224,512]{1,0:T(8,128)S(1)}, u32[]{:S(2)}) copy-start(f32[224,512]{1,0:T(8,128)S(1)} %reduce_sum.73) | copy-start | bytes 1376260
  474.8 6.7 copy-start.10
  475.3 6.3 copy-start.12
  475.7 5.8 copy-start.15
  481.6 100.4 %all-to-all-start.4 = ((f32[32,16,1536]{2,1,0:T(8,128)}), f32[32,16,1536]{2,1,0:T(8,128)S(1)}, u32[]{:S(2)}, u32[]{:S(2)}) async-start(f32[32,16,1536]{2,1,0:T(8,128)} %bitcast.116), calls=%async_computation.4 | async-start | bytes 6291456 | tf_op jit(solution)/shard_map/all_to_all | solution.py:30
  582.1 73.2 %copy-start.2 = (f32[224,512]{1,0:T(8,128)S(1)}, f32[224,512]{1,0:T(8,128)}, u32[]{:S(2)}) copy-start(f32[224,512]{1,0:T(8,128)} %copy-done.1) | copy-start | bytes 1376260
  582.8 19.5 %all-to-all-start.5 = ((f32[8,16,1]{1,2,0:T(1,128)}), f32[8,16,1]{1,2,0:T(1,128)S(1)}, u32[]{:S(2)}, u32[]{:S(2)}) async-start(f32[8,16,1]{1,2,0:T(1,128)} %broadcast_in_dim.11), calls=%async_computation.5 | async-start | bytes 8192 | tf_op jit(solution)/shard_map/all_to_all | solution.py:13
  587.7 164.1 %all-gather.2.cloned.1.call-start = ((), (), s32[]{:S(2)}) async-start(), calls=%async_computation.9 | async-start | bytes 3514368 | tf_op jit(solution)/shard_map/all_gather | solution.py:37
  602.5 54.6 %copy-start.20 = (f32[16,1536]{1,0:T(8,128)}, f32[16,1536]{1,0:T(8,128)S(1)}, u32[]{:S(2)}) copy-start(f32[16,1536]{1,0:T(8,128)S(1)} %broadcast_divide_fusion) | copy-start | bytes 294916
  603.3 54.1 %copy-start.7 = (f32[224,192]{0,1:T(8,128)S(1)}, f32[224,192]{0,1:T(8,128)}, u32[]{:S(2)}) copy-start(f32[224,192]{0,1:T(8,128)} %param.11) | copy-start | bytes 516100
  603.3 54.1 %copy-start.9 = (f32[224,192]{0,1:T(8,128)S(1)}, f32[224,192]{0,1:T(8,128)}, u32[]{:S(2)}) copy-start(f32[224,192]{0,1:T(8,128)} %param.10) | copy-start | bytes 516100
  657.4 94.4 %copy-start.11 = (f32[48,128]{1,0:T(8,128)S(1)}, f32[48,128]{1,0:T(8,128)}, u32[]{:S(2)}) copy-start(f32[48,128]{1,0:T(8,128)} %copy-done.10) | copy-start | bytes 73732
  657.4 94.4 %copy-start.13 = (f32[48,128]{1,0:T(8,128)S(1)}, f32[48,128]{1,0:T(8,128)}, u32[]{:S(2)}) copy-start(f32[48,128]{1,0:T(8,128)} %copy-done.12) | copy-start | bytes 73732
  657.4 94.4 %copy-start.16 = (f32[48,128]{1,0:T(8,128)S(1)}, f32[48,128]{1,0:T(8,128)}, u32[]{:S(2)}) copy-start(f32[48,128]{1,0:T(8,128)} %copy-done.15) | copy-start | bytes 73732
  657.5 94.4 %copy-start.19 = (f32[48,128]{1,0:T(8,128)S(1)}, f32[48,128]{1,0:T(8,128)}, u32[]{:S(2)}) copy-start(f32[48,128]{1,0:T(8,128)} %copy-done.18) | copy-start | bytes 73732
  699.0 57.5 %copy-start.21 = (f32[16,192]{1,0:T(8,128)}, f32[16,192]{1,0:T(8,128)S(1)}, u32[]{:S(2)}) copy-start(f32[16,192]{1,0:T(8,128)S(1)} %broadcast_divide_fusion.1) | copy-start | bytes 36868
  748.4 9.2 %copy-start.5 = (f32[48,1536]{1,0:T(8,128)S(1)}, f32[48,1536]{1,0:T(8,128)}, u32[]{:S(2)}) copy-start(f32[48,1536]{1,0:T(8,128)} %param.7) | copy-start | bytes 884740
  751.8 5.8 copy-start
  (5 other events, 12.7 us)
Sparse Core Ops, SparseCore 0:
  190.3 150.0 all-reduce.2
  603.4 89.4 all-gather.1
